TPU v7x, 32 devices: a whole 2x2x4 slice. The times are simulated.
32 devices in a mesh: ctx: 8 (over y, x, core), mp: 4 (over z).
Axes of the slice: x: 2, y: 2, z: 4, core: 2. Of those that a mesh axis runs over, the one named last changes fastest.
Arguments:
- queries: bfloat16 [128, 6144], P('ctx', 'mp'), may hold values from -9 to 9
- cache_keys: bfloat16 [8, 4096, 128], P('mp', 'ctx'), may hold values from -9 to 9, as said below
- cache_values: bfloat16 [8, 4096, 128], P('mp', 'ctx'), may hold values from -6 to 6, as said below
- new_keys: bfloat16 [8, 128, 128], P('mp', 'ctx'), may hold values from -6 to 6, as said below
- new_values: bfloat16 [8, 128, 128], P('mp', 'ctx'), may hold values from -6 to 6, as said below
- out_proj: bfloat16 [6144, 6144], P('mp', 'ctx'), may hold values from -3 to 3
- residual: bfloat16 [128, 6144], P('mp', 'ctx'), may hold values from -24 to 24
- norm_gain: bfloat16 [6144], replicated, may hold values from 0.5 to 1.5
- gate_proj: bfloat16 [8, 6144, 8192], P('ctx', None, 'mp'), may hold values from -0.078125 to 0.078125
- up_proj: bfloat16 [8, 6144, 8192], P('ctx', None, 'mp'), may hold values from -0.078125 to 0.078125
- down_proj: bfloat16 [8, 8192, 6144], P('ctx', 'mp'), may hold values from -0.09375 to 0.09375
- expert_ids: int32 [128, 2], replicated, may hold values from 0 to 7, all different within a row; in each aligned block of 128 rows (0 to 127, 128 to 255, ...) at most 64 rows name the same one
- route_logits: float32 [128, 2], replicated, may hold values from -6 to 6
Outputs:
- layer_out: bfloat16 [128, 6144], P('mp', 'ctx')
Inputs may be any that keep to these rules, and one draw needn't show every extreme that they name: `expert_ids`: each row names 2 different experts; at most 64 rows name one expert, a bound that some block reaches. `cache_keys`: slot s holds key head s * 1; slots of one key head are equal. `cache_values`: slot s holds value head s * 1; slots of one head are equal. `new_keys`: slot s holds key head s * 1; slots of one key head are equal. `new_values`: slot s holds value head s * 1; slots of one head are equal.
All inputs are finite; a program needn't handle non-finite values.
Results may differ from a plain program's by a relative error of at most 0.024.
Values may be sent and summed in bfloat16 or wider, within the bound.
No kernel may reach another device: no remote copies, remote signals or barrier semaphores. Data moves between devices by JAX's collectives and lax.ppermute only.
A program may use at most 128 MiB of HBM per device.

v0:
```python
import math
import jax
import jax.numpy as jnp
from jax import lax
from jax.sharding import PartitionSpec as P

D = 6144
EXPERTS = 8
TOP = 2
neg_big = -1e30
norm_eps = 1e-05


def route_slots(expert_ids):
    flat = expert_ids.reshape(-1)
    onehot = (flat[:, None] == jnp.arange(EXPERTS, dtype=jnp.int32)[None, :]).astype(jnp.int32)
    before = jnp.cumsum(onehot, axis=0, dtype=jnp.int32) - onehot
    return jnp.sum(before * onehot, axis=1, dtype=jnp.int32).reshape(expert_ids.shape)


def softmax_pieces(query_block, keys_local, values_local, allowed, scale):
    scores = (
        jnp.einsum("srd,skd->srk", query_block, keys_local, preferred_element_type=jnp.float32)
        * scale
    )
    scores = jnp.where(allowed[None, :, :], scores, neg_big)
    highest = jnp.max(scores, axis=2)
    expo = jnp.exp(scores - highest[:, :, None])
    denom = jnp.sum(expo, axis=2)
    summed = jnp.einsum(
        "srk,skd->srd", expo.astype(jnp.bfloat16), values_local, preferred_element_type=jnp.float32
    )
    return (highest, denom, summed)


def join_softmax(former, latter):
    highest = jnp.maximum(former[0], latter[0])
    right = jnp.exp(latter[0] - highest)
    denom = latter[1] * right
    summed = latter[2] * right[:, :, None]
    return (highest, denom, summed)


def on_device(
    queries,
    cache_keys,
    cache_values,
    new_keys,
    new_values,
    out_proj,
    residual,
    norm_gain,
    gate_proj,
    up_proj,
    down_proj,
    expert_ids,
    route_logits,
):
    ctx_count = lax.axis_size("ctx")
    mp_count = lax.axis_size("mp")
    ctx_index = lax.axis_index("ctx")
    mp_index = lax.axis_index("mp")
    tok_local = queries.shape[0]
    tokens = tok_local * ctx_count
    slot_local = cache_keys.shape[0]
    cache_local = cache_keys.shape[1]
    head_dim = cache_keys.shape[2]
    heads_local = queries.shape[1] // head_dim
    group_size = heads_local // slot_local
    width = cache_local + tok_local
    scale = 1.0 / math.sqrt(head_dim)
    d_local = out_proj.shape[1]
    key_value = jnp.stack(
        [
            jnp.concatenate([cache_keys, new_keys], axis=1),
            jnp.concatenate([cache_values, new_values], axis=1),
        ]
    )
    shaped = queries.reshape(tok_local, slot_local, group_size, head_dim)
    query_block = jnp.transpose(shaped, (1, 2, 0, 3)).reshape(
        slot_local, group_size * tok_local, head_dim
    )
    query_tok = ctx_index * tok_local + jnp.tile(jnp.arange(tok_local, dtype=jnp.int32), group_size)
    query_count = group_size * tok_local
    start_state = (
        jnp.full((slot_local, query_count), neg_big, jnp.float32),
        jnp.zeros((slot_local, query_count), jnp.float32),
        jnp.zeros((slot_local, query_count, head_dim), jnp.float32),
    )
    piece = lax.all_gather(key_value, "ctx", axis=2, tiled=True)
    position = jnp.arange(piece.shape[2], dtype=jnp.int32)
    shard = position // width
    within = position % width
    new_tok = shard * tok_local + within - cache_local
    allowed = (within[None, :] < cache_local) | (new_tok[None, :] <= query_tok[:, None])
    highest, denom, summed = join_softmax(
        start_state, softmax_pieces(query_block, piece[0], piece[1], allowed, scale)
    )
    shaped = (
        (summed / denom[:, :, None])
        .astype(jnp.bfloat16)
        .reshape(slot_local, group_size, tok_local, head_dim)
    )
    attn = jnp.transpose(shaped, (2, 0, 1, 3)).reshape(tok_local, heads_local * head_dim)
    projected = jnp.dot(
        lax.all_gather(attn, "ctx", axis=0, tiled=True),
        out_proj,
        preferred_element_type=jnp.float32,
    )
    res_rows = residual.shape[0]
    res_start = mp_index * res_rows
    current = lax.dynamic_slice_in_dim(projected, res_start, res_rows, 0)
    projected = lax.dynamic_update_slice_in_dim(
        projected, current + residual.astype(jnp.float32), res_start, 0
    )
    hidden = lax.psum(projected.astype(jnp.bfloat16), "mp")
    capacity = tokens * TOP // 4
    slots = route_slots(expert_ids)
    per_row = max(1, EXPERTS // mp_count)
    first_expert = mp_index * EXPERTS // mp_count
    own_expert = (mp_index * ctx_count + ctx_index) * EXPERTS // (ctx_count * mp_count)
    local = own_expert - first_expert
    row_experts = first_expert + jnp.arange(per_row, dtype=jnp.int32)
    match = expert_ids[None, :, :] == row_experts[:, None, None]
    place = jnp.where(match, slots[None, :, :], capacity)
    table = place[:, :, :, None] == jnp.arange(capacity, dtype=jnp.int32)[None, None, None, :]
    pick = jnp.any(table, axis=2)
    packed = jnp.einsum(
        "rtc,td->rcd", pick.astype(jnp.bfloat16), hidden, preferred_element_type=jnp.float32
    ).astype(jnp.bfloat16)
    gate_local = gate_proj[0]
    up_local = up_proj[0]
    down_local = down_proj[0]
    chosen = lax.dynamic_index_in_dim(
        lax.all_gather(packed, "ctx", axis=2, tiled=True), local, 0, keepdims=False
    )
    wide = chosen.astype(jnp.float32)
    gains = norm_gain.astype(jnp.float32)
    scaled = (wide * gains[None, :]).astype(jnp.bfloat16)
    gate_sum = jnp.dot(scaled, gate_local, preferred_element_type=jnp.float32)
    up_sum = jnp.dot(scaled, up_local, preferred_element_type=jnp.float32)
    gate_sum, up_sum, squares = (gate_sum, up_sum, jnp.sum(wide * wide, axis=1))
    rms = lax.rsqrt(squares / D + norm_eps)
    act = (jax.nn.silu(rms[:, None] * gate_sum) * (rms[:, None] * up_sum)).astype(jnp.bfloat16)
    part = lax.dot_general(
        down_local, act, (((0,), (1,)), ((), ())), preferred_element_type=jnp.float32
    )
    returned = lax.psum_scatter(
        jnp.concatenate(
            [jnp.where(local == which, part, 0.0) for which in range(per_row)], axis=1
        ).astype(jnp.bfloat16),
        "ctx",
        scatter_dimension=0,
        tiled=True,
    ).astype(jnp.float32)
    weights = jax.nn.softmax(route_logits, axis=1)
    combine = jnp.sum(jnp.where(table, weights[None, :, :, None], 0.0), axis=2)
    moe = jnp.einsum(
        "drc,rtc->td",
        returned.reshape(d_local, per_row, capacity),
        combine,
        precision=lax.Precision.HIGHEST,
        preferred_element_type=jnp.float32,
    )
    share = lax.psum_scatter(
        moe.astype(jnp.bfloat16), "mp", scatter_dimension=0, tiled=True
    ).astype(jnp.float32)
    own_hidden = lax.dynamic_slice_in_dim(hidden, res_start, res_rows, 0).astype(jnp.float32)
    return (own_hidden + share).astype(jnp.bfloat16)


def solution(mesh):
    placed = (
        P("ctx", "mp"),
        P("mp", "ctx", None),
        P("mp", "ctx", None),
        P("mp", "ctx", None),
        P("mp", "ctx", None),
        P("mp", "ctx"),
        P("mp", "ctx"),
        P(),
        P("ctx", None, "mp"),
        P("ctx", None, "mp"),
        P("ctx", "mp", None),
        P(),
        P(),
    )
    return jax.shard_map(
        on_device, mesh=mesh, in_specs=placed, out_specs=P("mp", "ctx"), check_vma=False
    )
```

profile of v0, /device:TPU:0, one launch (start us, length us, event | category | flops | bytes accessed | tf_op | source)
XLA Modules:
  0.0 234.1 jit_solution(1601538211125830650)
XLA Ops:
  6.5 1.3 maximum_bitcast_fusion
  7.8 0.9 pad_maximum_fusion.1
  8.8 0.8 copy.30
  9.8 0.6 reduce-window.6
  11.3 0.3 compare_or_fusion
  11.6 37.6 %all-gather.3.cloned.1.call-done = bf16[2,2,4224,128]{3,2,1,0:T(8,128)(2,1)} async-done(((bf16[2,2,528,128]{3,2,1,0:T(8,128)(2,1)}), bf16[2,2,4224,128]{3,2,1,0:T(8,128)(2,1)}) %all-gather.3.cloned.1.call-update) | async-done | bytes 4325392 | tf_op jit(solution)/shard_map/all_gather | solution.py:90
  49.3 2.8 %fusion.74 = (f32[2,96]{1,0:T(2,128)S(1)}, f32[2,96,4224]{2,1,0:T(8,128)S(1)}) fusion(bf16[2,96,128]{2,1,0:T(8,128)(2,1)S(1)} %bitcast.87, bf16[2,2,4224,128]{3,2,1,0:T(8,128)(2,1)} %all-gather.3.cloned.1.call-done, pred[96,4224]{1,0:T(8,128)(4,1)S(1)} %compare_or_fusion), kind=kOutput, calls=%fused_computation.88 | convolution fusion | flops 210050880 | bytes 5862144 | tf_op jit(solution)/shard_map/srd,skd->srk/dot_general | solution.py:23
  52.1 0.6 fusion.8
  52.7 0.8 fusion.36
  53.7 9.6 %all_gather.10 = bf16[128,1536]{1,0:T(8,128)(2,1)S(1)} all-gather(bf16[16,1536]{1,0:T(8,128)(2,1)S(1)} %reshape.152), channel_id=1, replica_groups=mesh['ctx'=8,'mp'=4] {'ctx'}, dimensions={0}, use_global_device_ids=true | all-gather | bytes 442368 | tf_op jit(solution)/shard_map/all_gather | solution.py:106
  63.2 0.5 fusion.81
  63.7 0.7 convert_element_type.59
  64.6 34.8 %all-reduce.2.cloned.1.call-done = bf16[128,768]{1,0:T(8,128)(2,1)} async-done(((bf16[128,768]{1,0:T(8,128)(2,1)}), bf16[128,768]{1,0:T(8,128)(2,1)}) %all-reduce.2.cloned.1.call-update) | async-done | bytes 196624 | tf_op jit(solution)/shard_map/psum | solution.py:116
  99.5 1.8 convolution_convert_fusion
  101.3 0.2 reduce-scatter.3.cloned.1.call-start
  101.6 25.4 %all-gather.5.cloned.1.call-done = bf16[2,64,6144]{2,1,0:T(8,128)(2,1)} async-done(((bf16[2,64,768]{2,1,0:T(8,128)(2,1)}), bf16[2,64,6144]{2,1,0:T(8,128)(2,1)}) %all-gather.5.cloned.1.call-update) | async-done | bytes 1572880 | tf_op jit(solution)/shard_map/all_gather | solution.py:135
  127.0 1.4 fusion.27
  128.4 13.7 %fusion.10 = f32[64,2048]{1,0:T(8,128)} fusion(bf16[1,6144,2048]{2,1,0:T(8,128)(2,1)} %param.21, f32[6144]{0:T(1024)S(1)} %convert_element_type.65, bf16[2,64,6144]{2,1,0:T(8,128)(2,1)} %all-gather.5.cloned.1.call-done, s32[]{:T(128)S(6)} %select_n.86, f32[64]{0:T(128)S(1)} %add_rsqrt_fusion), kind=kOutput, calls=%fused_computation.12 | convolution fusion | flops 1611923456 | bytes 26501380 | tf_op jit(solution)/shard_map/dot_general | solution.py:140
  142.1 21.4 %fusion.39 = (bf16[6144,64]{0,1:T(8,128)(2,1)S(1)}, bf16[6144,64]{0,1:T(8,128)(2,1)}) fusion(pred[]{:T(512)S(6)} %eq.77, pred[]{:T(512)S(6)} %eq.78, bf16[1,2048,6144]{2,1,0:T(8,128)(2,1)} %param.23, bf16[1,6144,2048]{2,1,0:T(8,128)(2,1)} %param.22, f32[6144]{0:T(1024)S(1)} %convert_element_type.65, bf16[2,64,6144]{2,1,0:T(8,128)(2,1)} %all-gather.5.cloned.1.call-done, ...), kind=kOutput, calls=%fused_computation.34 | convolution fusion | flops 3224109056 | bytes 53240072 | tf_op jit(solution)/shard_map/dot_general | solution.py:145
  163.5 2.4 %pad_maximum_fusion = bf16[6144,128]{0,1:T(8,128)(2,1)} fusion(bf16[6144,64]{0,1:T(8,128)(2,1)} %get-tuple-element.6, bf16[6144,64]{0,1:T(8,128)(2,1)S(1)} %get-tuple-element.5), kind=kLoop, calls=%fused_computation.25 | loop fusion | flops 3145728 | bytes 3145728 | tf_op jit(solution)/shard_map/concatenate | solution.py:149
  166.1 38.5 %reduce-scatter.3.cloned.1.call-done = bf16[768,128]{0,1:T(8,128)(2,1)} async-done(((bf16[6144,128]{0,1:T(8,128)(2,1)}), bf16[768,128]{0,1:T(8,128)(2,1)}) %reduce-scatter.3.cloned.1.call-update) | async-done | bytes 196624 | tf_op jit(solution)/shard_map/reduce_scatter | solution.py:148
  204.6 2.0 fusion.29
  206.6 19.6 %reduce-scatter.5.cloned.1.call-done = bf16[32,768]{1,0:T(8,128)(2,1)} async-done(((bf16[128,768]{1,0:T(8,128)(2,1)}), bf16[32,768]{1,0:T(8,128)(2,1)}) %reduce-scatter.5.cloned.1.call-update) | async-done | bytes 49168 | tf_op jit(solution)/shard_map/reduce_scatter | solution.py:165
  226.1 1.5 add_convert_fusion
  (56 shorter events, 1.6 us)
Async XLA Ops:
  6.5 56.7 %copy-start = (bf16[1536,768]{1,0:T(8,128)(2,1)S(1)}, bf16[1536,768]{1,0:T(8,128)(2,1)}, u32[]{:S(2)}) copy-start(bf16[1536,768]{1,0:T(8,128)(2,1)} %param.18) | copy-start | bytes 7077892
  6.5 4.6 %copy-start.2 = (bf16[16,1536]{1,0:T(8,128)(2,1)S(1)}, bf16[16,1536]{1,0:T(8,128)(2,1)}, u32[]{:S(2)}) copy-start(bf16[16,1536]{1,0:T(8,128)(2,1)} %param.13) | copy-start | bytes 147460
  6.5 42.7 %all-gather.3.cloned.1.call-start = ((), (), s32[]{:S(2)}) async-start(), calls=%async_computation.2 | async-start | bytes 4866048 | tf_op jit(solution)/shard_map/all_gather | solution.py:90
  8.7 90.8 %all-reduce.2.cloned.1.call-start = ((), (), s32[]{:S(2)}) async-start(), calls=%async_computation.3 | async-start | bytes 393216 | tf_op jit(solution)/shard_map/psum | solution.py:116
  49.3 3.4 %slice-start = ((s8[4325376]{0:T(1024)(128)(4,1)}), s8[4194304]{0:T(1024)(128)(4,1)S(1)}, s32[]{:S(2)}) async-start(s8[4325376]{0:T(1024)(128)(4,1)} %bitcast.89), calls=%async_computation.7 | async-start | bytes 8388608
  49.3 3.4 %slice-start.1 = ((s8[4325376]{0:T(1024)(128)(4,1)}), s8[131072]{0:T(1024)(128)(4,1)S(1)}, s32[]{:S(2)}) async-start(s8[4325376]{0:T(1024)(128)(4,1)} %bitcast.89), calls=%async_computation.8 | async-start | bytes 262144
  53.5 10.2 %copy-start.3 = (bf16[32,768]{1,0:T(8,128)(2,1)S(1)}, bf16[32,768]{1,0:T(8,128)(2,1)}, u32[]{:S(2)}) copy-start(bf16[32,768]{1,0:T(8,128)(2,1)} %param.19) | copy-start | bytes 147460
  53.5 11.0 %copy-start.6 = (s32[128,2]{0,1:T(2,128)S(1)}, s32[128,2]{0,1:T(2,128)}, u32[]{:S(2)}) copy-start(s32[128,2]{0,1:T(2,128)} %param.24) | copy-start | bytes 3076
  53.5 48.0 %copy-start.4 = (bf16[6144]{0:T(1024)(128)(2,1)S(1)}, bf16[6144]{0:T(1024)(128)(2,1)}, u32[]{:S(2)}) copy-start(bf16[6144]{0:T(1024)(128)(2,1)} %param.20) | copy-start | bytes 36868
  64.4 62.5 %all-gather.5.cloned.1.call-start = ((), (), s32[]{:S(2)}) async-start(), calls=%async_computation.4 | async-start | bytes 1769472 | tf_op jit(solution)/shard_map/all_gather | solution.py:135
  101.3 103.3 %reduce-scatter.3.cloned.1.call-start = ((), (), s32[]{:S(2)}) async-start(), calls=%async_computation.5 | async-start | bytes 1769472 | tf_op jit(solution)/shard_map/reduce_scatter | solution.py:148
  142.1 85.5 %copy-start.1 = (bf16[1536,768]{1,0:T(8,128)(2,1)S(1)}, bf16[1536,768]{1,0:T(8,128)(2,1)}, u32[]{:S(2)}) copy-start(bf16[1536,768]{1,0:T(8,128)(2,1)} %param.18) | copy-start | bytes 7077892
  163.5 2.5 %copy-start.5 = (f32[128,2]{0,1:T(2,128)S(1)}, f32[128,2]{0,1:T(2,128)}, u32[]{:S(2)}) copy-start(f32[128,2]{0,1:T(2,128)} %param.25) | copy-start | bytes 3076
  166.0 60.2 %reduce-scatter.5.cloned.1.call-start = ((), (), s32[]{:S(2)}) async-start(), calls=%async_computation.6 | async-start | bytes 245760 | tf_op jit(solution)/shard_map/reduce_scatter | solution.py:165
Sparse Core Ops, SparseCore 0:
  9.3 39.9 all-gather.2
  64.6 34.8 all-reduce.1
  101.5 25.3 all-gather.4
  166.1 38.4 reduce-scatter.2
  206.8 19.3 reduce-scatter.4
where the time goes:
time: 235 us; the launch traced here: 234 us
  waiting for transfers between devices  156 us (66%)
  matrix products  42.9 us (18%)
  between operations  13.4 us (6%)
  other arithmetic  10 us (4%)
  blocking collectives  9.55 us (4%)
    reduce_scatter x1, waiting for transfers between devices, on_device(): lax.psum_scatter(jnp.concatenate([jnp.where(local == which, part, 0.0) fo...  38.5 us
    all_gather x1, waiting for transfers between devices, on_device(): piece = lax.all_gather(key_value, 'ctx', axis=2, tiled=True)  37.6 us
    psum x1, waiting for transfers between devices, on_device(): hidden = lax.psum(projected.astype(jnp.bfloat16), 'mp')  34.8 us
    all_gather x1, waiting for transfers between devices, on_device(): lax.all_gather(packed, 'ctx', axis=2, tiled=True)  25.4 us
    dot_general x1, matrix products, on_device(): lax.dot_general(down_local, act, (((0,), (1,)), ((), ())), preferred_elem...  21.4 us
    reduce_scatter x1, waiting for transfers between devices, on_device(): lax.psum_scatter(moe.astype(jnp.bfloat16), 'mp', scatter_dimension=0, til...  19.6 us
    dot_general x1, matrix products, on_device(): gate_sum = jnp.dot(scaled, gate_local, preferred_element_type=jnp.float32)  13.7 us
    all_gather x1, blocking collectives, on_device(): lax.all_gather(attn, 'ctx', axis=0, tiled=True)  9.55 us
  transfers between devices with their start and end apart: 5, of which 5 were waited for; matrix products, arithmetic and copies ran while one was open for 1% of the time, Pallas kernels for 0%

commit v1 on v0

--- a/solution.py
+++ b/solution.py
@@ -113,7 +113,7 @@
     projected = lax.dynamic_update_slice_in_dim(
         projected, current + residual.astype(jnp.float32), res_start, 0
     )
-    hidden = lax.psum(projected.astype(jnp.bfloat16), "mp")
+    hidden = jnp.sum(lax.all_gather(projected.astype(jnp.bfloat16), "mp"), axis=0)
     capacity = tokens * TOP // 4
     slots = route_slots(expert_ids)
     per_row = max(1, EXPERTS // mp_count)

time: 235 us -> 216 us (0.919)
  waiting for transfers between devices: 156 us -> 120 us
  blocking collectives: 9.55 us -> 29.1 us
    psum x1 -> x0, waiting for transfers between devices: 34.8 us -> none  [on_device(): hidden = lax.psum(projected.astype(jnp.bfloat16), 'mp')]
    all_gather x0 -> x1, blocking collectives: none -> 19.5 us  [on_device(): lax.all_gather(projected.astype(jnp.bfloat16), 'mp')]
  transfers between devices with their start and end apart: 5 -> 4, of which waited for: 5 -> 4; matrix products, arithmetic and copies ran while one was open for 1% -> 1% of each run, Pallas kernels for 0% -> 0%
where the time goes in v1:
time: 216 us
  waiting for transfers between devices  120 us (56%)
  matrix products  42 us (19%)
  blocking collectives  29.1 us (13%)
  between operations  13.4 us (6%)
  other arithmetic  9.46 us (4%)
    reduce_scatter x1, waiting for transfers between devices, on_device(): lax.psum_scatter(jnp.concatenate([jnp.where(local == which, part, 0.0) fo...  38.5 us
    all_gather x1, waiting for transfers between devices, on_device(): piece = lax.all_gather(key_value, 'ctx', axis=2, tiled=True)  37.5 us
    all_gather x1, waiting for transfers between devices, on_device(): lax.all_gather(packed, 'ctx', axis=2, tiled=True)  24.1 us
    dot_general x1, matrix products, on_device(): lax.dot_general(down_local, act, (((0,), (1,)), ((), ())), preferred_elem...  21.4 us
    all_gather x1, blocking collectives, on_device(): lax.all_gather(projected.astype(jnp.bfloat16), 'mp')  19.5 us
    reduce_scatter x1, waiting for transfers between devices, on_device(): lax.psum_scatter(moe.astype(jnp.bfloat16), 'mp', scatter_dimension=0, til...  19.5 us
    dot_general x1, matrix products, on_device(): gate_sum = jnp.dot(scaled, gate_local, preferred_element_type=jnp.float32)  13.7 us
    all_gather x1, blocking collectives, on_device(): lax.all_gather(attn, 'ctx', axis=0, tiled=True)  9.54 us
  transfers between devices with their start and end apart: 4, of which 4 were waited for; matrix products, arithmetic and copies ran while one was open for 1% of the time, Pallas kernels for 0%

profile of v1, /device:TPU:0, one launch (start us, length us, event | category | flops | bytes accessed | tf_op | source)
XLA Modules:
  0.0 215.6 jit_solution(14895729790930824606)
XLA Ops:
  6.5 1.3 maximum_bitcast_fusion
  7.8 0.9 pad_maximum_fusion.1
  8.8 0.8 copy.30
  9.9 0.6 reduce-window.6
  10.5 0.2 slice_reduce_fusion
  11.4 0.3 compare_or_fusion
  11.8 37.5 %all-gather.4.cloned.1.call-done = bf16[2,2,4224,128]{3,2,1,0:T(8,128)(2,1)} async-done(((bf16[2,2,528,128]{3,2,1,0:T(8,128)(2,1)}), bf16[2,2,4224,128]{3,2,1,0:T(8,128)(2,1)}) %all-gather.4.cloned.1.call-update) | async-done | bytes 4325392 | tf_op jit(solution)/shard_map/all_gather | solution.py:90
  49.3 2.8 %fusion.74 = (f32[2,96]{1,0:T(2,128)S(1)}, f32[2,96,4224]{2,1,0:T(8,128)S(1)}) fusion(bf16[2,96,128]{2,1,0:T(8,128)(2,1)S(1)} %bitcast.89, bf16[2,2,4224,128]{3,2,1,0:T(8,128)(2,1)} %all-gather.4.cloned.1.call-done, pred[96,4224]{1,0:T(8,128)(4,1)S(1)} %compare_or_fusion), kind=kOutput, calls=%fused_computation.88 | convolution fusion | flops 210050880 | bytes 5862144 | tf_op jit(solution)/shard_map/srd,skd->srk/dot_general | solution.py:23
  52.1 0.6 fusion.8
  52.7 0.7 fusion.36
  53.6 9.5 %all_gather.16 = bf16[128,1536]{1,0:T(8,128)(2,1)S(1)} all-gather(bf16[16,1536]{1,0:T(8,128)(2,1)S(1)} %reshape.152), channel_id=1, replica_groups=mesh['ctx'=8,'mp'=4] {'ctx'}, dimensions={0}, use_global_device_ids=true | all-gather | bytes 442368 | tf_op jit(solution)/shard_map/all_gather | solution.py:106
  63.1 0.5 fusion.81
  63.7 19.5 %all-gather = bf16[512,768]{1,0:T(8,128)(2,1)S(1)} all-gather(bf16[128,768]{1,0:T(8,128)(2,1)S(1)} %convert_element_type.61), channel_id=2, replica_groups=mesh['ctx'=8,'mp'=4] {'mp'}, dimensions={0}, use_global_device_ids=true | all-gather | bytes 983040 | tf_op jit(solution)/shard_map/all_gather | solution.py:116
  83.3 0.9 convolution_convert_fusion
  84.2 0.2 reduce-scatter.3.cloned.1.call-start
  84.5 24.1 %all-gather.6.cloned.1.call-done = bf16[2,64,6144]{2,1,0:T(8,128)(2,1)} async-done(((bf16[2,64,768]{2,1,0:T(8,128)(2,1)}), bf16[2,64,6144]{2,1,0:T(8,128)(2,1)}) %all-gather.6.cloned.1.call-update) | async-done | bytes 1572880 | tf_op jit(solution)/shard_map/all_gather | solution.py:135
  108.5 1.4 fusion.27
  110.0 13.7 %fusion.10 = f32[64,2048]{1,0:T(8,128)} fusion(bf16[1,6144,2048]{2,1,0:T(8,128)(2,1)} %param.21, f32[6144]{0:T(1024)S(1)} %convert_element_type.67, bf16[2,64,6144]{2,1,0:T(8,128)(2,1)} %all-gather.6.cloned.1.call-done, s32[]{:T(128)S(6)} %select_n.86, f32[64]{0:T(128)S(1)} %add_rsqrt_fusion), kind=kOutput, calls=%fused_computation.12 | convolution fusion | flops 1611923456 | bytes 26501380 | tf_op jit(solution)/shard_map/dot_general | solution.py:140
  123.7 21.4 %fusion.39 = (bf16[6144,64]{0,1:T(8,128)(2,1)S(1)}, bf16[6144,64]{0,1:T(8,128)(2,1)}) fusion(pred[]{:T(512)S(6)} %eq.77, pred[]{:T(512)S(6)} %eq.78, bf16[1,2048,6144]{2,1,0:T(8,128)(2,1)} %param.23, bf16[1,6144,2048]{2,1,0:T(8,128)(2,1)} %param.22, f32[6144]{0:T(1024)S(1)} %convert_element_type.67, bf16[2,64,6144]{2,1,0:T(8,128)(2,1)} %all-gather.6.cloned.1.call-done, ...), kind=kOutput, calls=%fused_computation.34 | convolution fusion | flops 3224109056 | bytes 53240072 | tf_op jit(solution)/shard_map/dot_general | solution.py:145
  145.1 2.4 %pad_maximum_fusion = bf16[6144,128]{0,1:T(8,128)(2,1)} fusion(bf16[6144,64]{0,1:T(8,128)(2,1)} %get-tuple-element.6, bf16[6144,64]{0,1:T(8,128)(2,1)S(1)} %get-tuple-element.5), kind=kLoop, calls=%fused_computation.25 | loop fusion | flops 3145728 | bytes 3145728 | tf_op jit(solution)/shard_map/concatenate | solution.py:149
  147.7 38.5 %reduce-scatter.3.cloned.1.call-done = bf16[768,128]{0,1:T(8,128)(2,1)} async-done(((bf16[6144,128]{0,1:T(8,128)(2,1)}), bf16[768,128]{0,1:T(8,128)(2,1)}) %reduce-scatter.3.cloned.1.call-update) | async-done | bytes 196624 | tf_op jit(solution)/shard_map/reduce_scatter | solution.py:148
  186.2 2.0 fusion.29
  188.2 19.5 %reduce-scatter.5.cloned.1.call-done = bf16[32,768]{1,0:T(8,128)(2,1)} async-done(((bf16[128,768]{1,0:T(8,128)(2,1)}), bf16[32,768]{1,0:T(8,128)(2,1)}) %reduce-scatter.5.cloned.1.call-update) | async-done | bytes 49168 | tf_op jit(solution)/shard_map/reduce_scatter | solution.py:165
  207.6 1.4 add_convert_fusion
  (55 shorter events, 1.5 us)
Async XLA Ops:
  6.5 56.6 %copy-start = (bf16[1536,768]{1,0:T(8,128)(2,1)S(1)}, bf16[1536,768]{1,0:T(8,128)(2,1)}, u32[]{:S(2)}) copy-start(bf16[1536,768]{1,0:T(8,128)(2,1)} %param.18) | copy-start | bytes 7077892
  6.5 4.8 %copy-start.6 = (s32[128,2]{0,1:T(2,128)S(1)}, s32[128,2]{0,1:T(2,128)}, u32[]{:S(2)}) copy-start(s32[128,2]{0,1:T(2,128)} %param.24) | copy-start | bytes 3076
  6.5 4.6 %copy-start.2 = (bf16[16,1536]{1,0:T(8,128)(2,1)S(1)}, bf16[16,1536]{1,0:T(8,128)(2,1)}, u32[]{:S(2)}) copy-start(bf16[16,1536]{1,0:T(8,128)(2,1)} %param.13) | copy-start | bytes 147460
  6.5 42.7 %all-gather.4.cloned.1.call-start = ((), (), s32[]{:S(2)}) async-start(), calls=%async_computation.2 | async-start | bytes 4866048 | tf_op jit(solution)/shard_map/all_gather | solution.py:90
  8.7 99.8 %all-gather.6.cloned.1.call-start = ((), (), s32[]{:S(2)}) async-start(), calls=%async_computation.3 | async-start | bytes 1769472 | tf_op jit(solution)/shard_map/all_gather | solution.py:135
  49.3 3.4 %slice-start = ((s8[4325376]{0:T(1024)(128)(4,1)}), s8[4194304]{0:T(1024)(128)(4,1)S(1)}, s32[]{:S(2)}) async-start(s8[4325376]{0:T(1024)(128)(4,1)} %bitcast.91), calls=%async_computation.6 | async-start | bytes 8388608
  49.3 3.4 %slice-start.1 = ((s8[4325376]{0:T(1024)(128)(4,1)}), s8[131072]{0:T(1024)(128)(4,1)S(1)}, s32[]{:S(2)}) async-start(s8[4325376]{0:T(1024)(128)(4,1)} %bitcast.91), calls=%async_computation.7 | async-start | bytes 262144
  53.4 10.2 %copy-start.3 = (bf16[32,768]{1,0:T(8,128)(2,1)S(1)}, bf16[32,768]{1,0:T(8,128)(2,1)}, u32[]{:S(2)}) copy-start(bf16[32,768]{1,0:T(8,128)(2,1)} %param.19) | copy-start | bytes 147460
  63.1 21.4 %copy-start.4 = (bf16[6144]{0:T(1024)(128)(2,1)S(1)}, bf16[6144]{0:T(1024)(128)(2,1)}, u32[]{:S(2)}) copy-start(bf16[6144]{0:T(1024)(128)(2,1)} %param.20) | copy-start | bytes 36868
  84.2 102.0 %reduce-scatter.3.cloned.1.call-start = ((), (), s32[]{:S(2)}) async-start(), calls=%async_computation.4 | async-start | bytes 1769472 | tf_op jit(solution)/shard_map/reduce_scatter | solution.py:148
  123.7 85.4 %copy-start.1 = (bf16[1536,768]{1,0:T(8,128)(2,1)S(1)}, bf16[1536,768]{1,0:T(8,128)(2,1)}, u32[]{:S(2)}) copy-start(bf16[1536,768]{1,0:T(8,128)(2,1)} %param.18) | copy-start | bytes 7077892
  145.1 2.5 %copy-start.5 = (f32[128,2]{0,1:T(2,128)S(1)}, f32[128,2]{0,1:T(2,128)}, u32[]{:S(2)}) copy-start(f32[128,2]{0,1:T(2,128)} %param.25) | copy-start | bytes 3076
  147.5 60.1 %reduce-scatter.5.cloned.1.call-start = ((), (), s32[]{:S(2)}) async-start(), calls=%async_computation.5 | async-start | bytes 245760 | tf_op jit(solution)/shard_map/reduce_scatter | solution.py:165
Sparse Core Ops, SparseCore 0:
  9.3 39.9 all-gather.3
  84.3 24.1 all-gather.5
  147.7 38.4 reduce-scatter.2
  188.3 19.3 reduce-scatter.4
